TPU v7x, 32 devices: a whole 2x2x4 slice. The times are simulated.
32 devices in a mesh: strike: 8 (over z, y), depth: 4 (over x, core).
Axes of the slice: x: 2, y: 2, z: 4, core: 2. Of those that a mesh axis runs over, the one named last changes fastest.
Arguments:
- velocity: float32 [3, 128, 64, 256], P(None, 'strike', 'depth'), may hold values from -6 to 6
- stress: float32 [6, 128, 64, 256], P(None, 'strike', 'depth'), may hold values from -6 to 6
- material: int32 [128, 64, 256], P('strike', 'depth'), may hold values from 0 to 3
- patch_order: int32 [48], replicated, may hold values from 0 to 47, each once
- fault_params: float32 [4, 64, 48], P(None, 'depth', 'strike'), may hold values from -5 to 5, as said below
Outputs:
- velocity_out: float32 [3, 128, 64, 256], P(None, 'strike', 'depth')
- slip_rate: float32 [64, 48], P('depth', 'strike')
Inputs may be any that keep to these rules, and one draw needn't show every extreme that they name: `fault_params`: row 0 in 0.3 to 1.2, row 1 in -0.5 to 1.5, row 2 in 1 to 3, row 3 in -5 to 5. `patch_order`: each fault column exactly once.
All inputs are finite; a program needn't handle non-finite values.
Results may differ from a plain program's by a relative error of at most 0.0003.
Values sent between devices are 32-bit elements; how exact they have to be, the bound alone decides.
A program may use at most 64 MiB of HBM per device.

v0:
```python
import jax
import jax.numpy as jnp
from jax import lax
from jax.sharding import PartitionSpec as P

NEWTON = 8


BUOY = (1.0, 0.8, 0.6, 1.25)
C_ONE = 9.0 / 8.0
C_TWO = -1.0 / 24.0


def with_halo(value, sides, width):
    for axis, dim in sides:
        size, length = (lax.axis_size(axis), value.shape[dim])
        up = [(i, (i + 1) % size) for i in range(size - 1)]
        down = [(j, i) for i, j in up]
        last = lax.slice_in_dim(value, length - width, length, axis=dim)
        first = lax.slice_in_dim(value, 0, width, axis=dim)
        before = lax.ppermute(last, axis, up)
        after = lax.ppermute(first, axis, down)
        value = jnp.concatenate([before, value, after], axis=dim)
    return value


def inverse_sinh(value):
    magnitude = jnp.log(jnp.abs(value) + jnp.sqrt(1.0 + value * value))
    return jnp.where(value < 0, -magnitude, magnitude)


def minus_padded(padded, axis):
    width = padded.shape[axis] - 4

    def part(offset):
        return lax.slice_in_dim(padded, 2 + offset, 2 + offset + width, axis=axis)

    return C_ONE * (part(0) - part(-1)) + C_TWO * (part(1) - part(-2))


def plus_padded(padded, axis):
    width = padded.shape[axis] - 4

    def part(offset):
        return lax.slice_in_dim(padded, 2 + offset, 2 + offset + width, axis=axis)

    return C_ONE * (part(1) - part(0)) + C_TWO * (part(2) - part(-1))


def pad_normal(field):
    return jnp.pad(field, ((0, 0), (0, 0), (2, 2)))


def friction(tau_trial, params):
    coef, psi, normal_stress, background = (params[0], params[1], params[2], params[3])
    tau_total = tau_trial + background
    half_q = 0.5 * jnp.exp(psi / coef)
    scale = normal_stress * coef
    rate = jnp.zeros_like(tau_total)
    for step in range(NEWTON):
        arg_val = rate * half_q
        resid = tau_total - rate - scale * inverse_sinh(arg_val)
        slope = -1.0 - scale * half_q / jnp.sqrt(1.0 + arg_val * arg_val)
        rate = rate - 0.35 * resid / slope
    return rate


def per_device(velocity, stress, material, patch_order, fault_params):
    cx, cz, ny = (stress.shape[1], stress.shape[2], stress.shape[3])
    row = ny // 2
    stacked = jnp.stack([stress[0], stress[2], stress[3], stress[4], stress[5]])
    padded = with_halo(stacked, (("strike", 1), ("depth", 2)), 2)
    x_part = padded[:, :, 2:-2]
    z_part = padded[:, 2:-2, :]
    x_sxx, x_sxy, x_sxz = (x_part[0], x_part[2], x_part[3])
    z_sxz, z_syz, z_szz = (z_part[3], z_part[4], z_part[1])
    buoyancy = jnp.zeros(material.shape, jnp.float32)
    for index in range(4):
        buoyancy = buoyancy + (material == index).astype(jnp.float32) * BUOY[index]
    dxx = minus_padded(x_sxx, 0)
    vx = velocity[0] + 0.25 * buoyancy * (
        dxx + minus_padded(pad_normal(stress[3]), 2) + minus_padded(z_sxz, 1)
    )
    vy = velocity[1] + 0.25 * buoyancy * (
        plus_padded(x_sxy, 0) + plus_padded(pad_normal(stress[1]), 2) + minus_padded(z_syz, 1)
    )
    vz = velocity[2] + 0.25 * buoyancy * (
        plus_padded(x_sxz, 0) + plus_padded(pad_normal(stress[5]), 2) + plus_padded(z_szz, 1)
    )
    fault_cols = patch_order.shape[0]
    n_strike = lax.axis_size("strike")
    strike_pos = lax.axis_index("strike")
    first_tile = n_strike // 4
    fault_tiles = fault_cols // cx
    inside = jnp.logical_and(strike_pos >= first_tile, strike_pos < first_tile + fault_tiles)
    offset = jnp.clip(strike_pos - first_tile, 0, fault_tiles - 1) * cx
    selector = (patch_order[:, None] == jnp.arange(fault_cols, dtype=jnp.int32)[None, :]).astype(
        jnp.float32
    )
    local_traction = (stress[3, :, :, row] + 0.5 * dxx[:, :, row]).T
    blank = jnp.zeros((cz, fault_cols), jnp.float32)
    masked = jnp.where(inside, local_traction, 0.0)
    owned = lax.psum_scatter(
        jnp.dot(
            lax.dynamic_update_slice(blank, masked, (jnp.int32(0), offset)),
            selector.T,
            precision=lax.Precision.HIGHEST,
            preferred_element_type=jnp.float32,
        ),
        "strike",
        scatter_dimension=1,
        tiled=True,
    )
    slip_own = friction(owned, fault_params)
    slip_all = lax.all_gather(slip_own, "strike", axis=1, tiled=True)
    slip_tile = lax.dynamic_slice(
        jnp.dot(
            slip_all, selector, precision=lax.Precision.HIGHEST, preferred_element_type=jnp.float32
        ),
        (jnp.int32(0), offset),
        (cz, cx),
    )
    slip_planar = slip_tile.T
    plus_side = vx[:, :, row]
    minus_side = vx[:, :, row - 1]
    middle = 0.5 * (plus_side + minus_side)
    vx = vx.at[:, :, row].set(jnp.where(inside, middle + 0.5 * slip_planar, plus_side))
    vx = vx.at[:, :, row - 1].set(jnp.where(inside, middle - 0.5 * slip_planar, minus_side))
    return (jnp.stack([vx, vy, vz]), slip_own)


def solution(mesh):
    return jax.shard_map(
        per_device,
        mesh=mesh,
        in_specs=(
            P(None, "strike", "depth", None),
            P(None, "strike", "depth", None),
            P("strike", "depth", None),
            P(),
            P(None, "depth", "strike"),
        ),
        out_specs=(P(None, "strike", "depth", None), P("depth", "strike")),
        check_vma=False,
    )
```

profile of v0, /device:TPU:2, one launch (start us, length us, event | category | flops | bytes accessed | tf_op | source)
XLA Modules:
  0.0 105.1 jit_solution(18227903959645477159)
XLA Ops:
  0.6 0.0 copy-start
  0.6 2.1 %slice_bitcast_fusion.2 = (f32[16,16,256]{2,1,0:T(8,128)}, f32[16,16,256]{2,1,0:T(8,128)S(1)}, f32[1,16,16,256]{3,2,1,0:T(8,128)S(1)}, f32[16,16,256]{2,1,0:T(8,128)S(1)}) fusion(f32[6,16,16,256]{3,2,1,0:T(8,128)} %param.10), kind=kLoop, calls=%fused_computation.87 | loop fusion | bytes 2097152 | tf_op jit(solution)/shard_map/squeeze | solution.py:82
  2.7 0.0 copy-done
  2.7 0.0 copy-start.6
  2.7 0.1 slice.262
  2.8 0.0 copy-start.4
  2.8 1.3 %collective-permute-start.1 = (f32[5,2,16,256]{3,2,1,0:T(8,128)S(1)}, f32[5,2,16,256]{3,2,1,0:T(8,128)S(1)}, u32[]{:S(2)}, u32[]{:S(2)}) collective-permute-start(f32[5,2,16,256]{3,2,1,0:T(8,128)S(1)} %get-tuple-element.42), channel_id=1, source_target_pairs={{4,0},{8,4},{12,8},{16,12},{20,16},{24,20},{28,24},{5,1},{9,5},{13... | collective-permute-start | bytes 491528 | tf_op jit(solution)/shard_map/ppermute | solution.py:22
  4.1 4.6 %collective-permute-start = (f32[5,2,16,256]{3,2,1,0:T(8,128)S(1)}, f32[5,2,16,256]{3,2,1,0:T(8,128)S(1)}, u32[]{:S(2)}, u32[]{:S(2)}) collective-permute-start(f32[5,2,16,256]{3,2,1,0:T(8,128)S(1)} %get-tuple-element.41), channel_id=1, source_target_pairs={{0,4},{4,8},{8,12},{12,16},{16,20},{20,24},{24,28},{1,5},{5,9},{9,... | collective-permute-start | bytes 491528 | tf_op jit(solution)/shard_map/ppermute | solution.py:21
  8.7 0.2 copy.200
  8.9 0.0 copy-done.6
  8.9 0.6 dynamic-slice.16
  10.1 0.5 collective-permute-done.1
  10.7 3.4 %collective-permute-done = f32[5,2,16,256]{3,2,1,0:T(8,128)S(1)} collective-permute-done((f32[5,2,16,256]{3,2,1,0:T(8,128)S(1)}, f32[5,2,16,256]{3,2,1,0:T(8,128)S(1)}, u32[]{:S(2)}, u32[]{:S(2)}) %collective-permute-start) | collective-permute-done | bytes 163872 | tf_op jit(solution)/shard_map/ppermute | solution.py:21
  14.1 0.1 pad_maximum_fusion.13
  14.3 2.1 %collective-permute-start.3 = (f32[5,20,2,256]{3,2,1,0:T(2,128)S(1)}, f32[5,20,2,256]{3,2,1,0:T(2,128)S(1)}, u32[]{:S(2)}, u32[]{:S(2)}) collective-permute-start(f32[5,20,2,256]{3,2,1,0:T(2,128)S(1)} %get-tuple-element.36), channel_id=1, source_target_pairs={{1,0},{2,1},{3,2},{5,4},{6,5},{7,6},{9,8},{10,9},{11,10},{13,12},{... | collective-permute-start | bytes 614408 | tf_op jit(solution)/shard_map/ppermute | solution.py:22
  16.3 2.3 %collective-permute-start.2 = (f32[5,20,2,256]{3,2,1,0:T(2,128)S(1)}, f32[5,20,2,256]{3,2,1,0:T(2,128)S(1)}, u32[]{:S(2)}, u32[]{:S(2)}) collective-permute-start(f32[5,20,2,256]{3,2,1,0:T(2,128)S(1)} %get-tuple-element.35), channel_id=1, source_target_pairs={{0,1},{1,2},{2,3},{4,5},{5,6},{6,7},{8,9},{9,10},{10,11},{12,13},{... | collective-permute-start | bytes 614408 | tf_op jit(solution)/shard_map/ppermute | solution.py:21
  18.6 0.0 copy-done.4
  18.6 0.0 copy-start.1
  18.7 0.0 copy-start.2
  18.7 0.9 collective-permute-done.3
  19.6 3.8 %collective-permute-done.2 = f32[5,20,2,256]{3,2,1,0:T(2,128)S(1)} collective-permute-done((f32[5,20,2,256]{3,2,1,0:T(2,128)S(1)}, f32[5,20,2,256]{3,2,1,0:T(2,128)S(1)}, u32[]{:S(2)}, u32[]{:S(2)}) %collective-permute-start.2) | collective-permute-done | bytes 204832 | tf_op jit(solution)/shard_map/ppermute | solution.py:21
  23.4 0.2 maximum_bitcast_fusion.1
  23.6 0.0 copy-done.1
  23.6 0.0 copy-done.2
  23.6 0.0 copy-start.5
  23.6 1.3 %fusion.7 = (f32[16,16,256]{2,1,0:T(8,128)S(1)}, f32[16,16,256]{2,1,0:T(8,128)S(1)}) fusion(f32[16,16,256]{2,1,0:T(8,128)S(1)} %copy-done.2, f32[16,20,256]{2,1,0:T(8,128)S(1)} %get-tuple-element.32, f32[3,16,16,256]{3,2,1,0:T(8,128)} %param.9, s32[16,16,256]{2,1,0:T(8,128)S(1)} %copy-done.1, f32[4,16,16,256]{3,2,1,0:T(8,128)S(1)} %slice.262, ...), kind=kLoop, calls=%fused_computation.24 | loop fusion | flops 2424832 | bytes 3997696 | tf_op jit(solution)/shard_map/add | solution.py:81
  25.0 0.8 fusion.108
  25.7 1.1 %copy.199 = f32[16,16,1]{0,1,2:T(8,128)S(1)} copy(f32[16,16,1]{2,1,0:T(8,128)} %get-tuple-element.43) | data formatting | bytes 2048 | tf_op jit(solution)/shard_map/squeeze | solution.py:125
  26.8 1.1 %copy.193 = f32[16,16,1]{0,1,2:T(8,128)S(1)} copy(f32[16,16,1]{2,1,0:T(8,128)} %get-tuple-element.51) | data formatting | bytes 2048 | tf_op jit(solution)/shard_map/mul | solution.py:100
  27.9 0.2 dynamic_update_slice.3
  28.1 0.0 copy-done.5
  28.1 0.2 fusion.54
  28.3 36.0 %all-reduce.3 = f32[16,48]{0,1:T(8,128)S(1)} all-reduce(f32[16,48]{0,1:T(8,128)S(1)} %fusion.54), channel_id=2, replica_groups=mesh['strike'=8,'depth'=4] {'strike'}, use_global_device_ids=true, to_apply=%region_0.1.clone | all-reduce | flops 768 | bytes 6144
  64.3 0.2 fusion.103
  64.6 0.0 copy-start.3
  64.6 30.6 %all-gather = f32[8,6,16]{2,1,0:T(8,128)S(1)} all-gather(f32[1,6,16]{2,1,0:T(8,128)S(1)} %bitcast.174), channel_id=1, replica_groups=mesh['strike'=8,'depth'=4] {'strike'}, dimensions={0}, use_global_device_ids=true | all-gather | bytes 3456 | tf_op jit(solution)/shard_map/all_gather | solution.py:115
  95.2 0.2 fusion.53
  95.4 1.1 %copy.198 = f32[16,16,1]{0,1,2:T(8,128)S(1)} copy(f32[16,16,1]{2,1,0:T(8,128)} %get-tuple-element.44) | data formatting | bytes 2048 | tf_op jit(solution)/shard_map/squeeze | solution.py:124
  96.5 0.1 fusion.58
  96.6 0.8 copy.189
  97.4 0.8 copy.192
  98.2 1.0 scatter.6
  99.2 2.1 %scatter.9 = f32[1,16,16,256]{3,2,1,0:T(8,128)S(1)} dynamic-update-slice(f32[1,16,16,256]{3,2,1,0:T(8,128)S(1)} %scatter.6, f32[1,16,16,1]{3,2,1,0:T(8,128)} %copy.192, s32[]{:T(128)} %constant.89.clone.1, s32[]{:T(128)} %constant.89.clone.1, s32[]{:T(128)} %constant.89.clone.1, s32[]{:T(128)} %constant.111.clone.1) | dynamic-update-slice | bytes 2052 | tf_op jit(solution)/shard_map/scatter | solution.py:128
  101.4 1.4 %fusion.27 = f32[1,16,16,256]{3,2,1,0:T(8,128)S(1)} fusion(f32[16,16,256]{2,1,0:T(8,128)S(1)} %get-tuple-element.40, f32[16,20,256]{2,1,0:T(8,128)S(1)} %get-tuple-element.34, f32[5,2,16,256]{3,2,1,0:T(8,128)S(1)} %collective-permute-done, f32[4,16,16,256]{3,2,1,0:T(8,128)S(1)} %slice.262, f32[1,16,16,256]{3,2,1,0:T(8,128)S(1)} %get-tuple-element.39, ...), kind=kLoop, calls=%fused_computation.44 | loop fusion | flops 2424832 | bytes 3997696 | tf_op jit(solution)/shard_map/stack | solution.py:129
  102.8 0.0 copy-done.3
  102.8 1.4 %fusion.17 = f32[1,16,16,256]{3,2,1,0:T(8,128)S(1)} fusion(f32[16,16,256]{2,1,0:T(8,128)S(1)} %get-tuple-element.38, f32[16,20,256]{2,1,0:T(8,128)S(1)} %get-tuple-element.33, f32[5,2,16,256]{3,2,1,0:T(8,128)S(1)} %collective-permute-done, f32[4,16,16,256]{3,2,1,0:T(8,128)S(1)} %slice.262, f32[1,16,16,256]{3,2,1,0:T(8,128)S(1)} %get-tuple-element.39, ...), kind=kLoop, calls=%fused_computation.34 | loop fusion | flops 2424832 | bytes 3997696 | tf_op jit(solution)/shard_map/stack | solution.py:129
  104.2 0.9 pad_maximum_fusion
  (6 shorter events, 0.1 us)
Async XLA Ops:
  0.6 2.1 %copy-start = (f32[6,16,16,256]{3,2,1,0:T(8,128)S(1)}, f32[6,16,16,256]{3,2,1,0:T(8,128)}, u32[]{:S(2)}) copy-start(f32[6,16,16,256]{3,2,1,0:T(8,128)} %param.10) | copy-start | bytes 4718596
  2.7 6.2 %copy-start.6 = (u32[32]{0:T(128)S(1)}, u32[32]{0:T(128)}, u32[]{:S(2)}) copy-start(u32[32]{0:T(128)} %constant.121) | copy-start | bytes 388
  2.8 15.8 %copy-start.4 = (f32[4,16,6]{1,0,2:T(4,128)S(1)}, f32[4,16,6]{1,0,2:T(4,128)}, u32[]{:S(2)}) copy-start(f32[4,16,6]{1,0,2:T(4,128)} %param.13) | copy-start | bytes 4612
  2.8 7.8 %collective-permute-start.1 = (f32[5,2,16,256]{3,2,1,0:T(8,128)S(1)}, f32[5,2,16,256]{3,2,1,0:T(8,128)S(1)}, u32[]{:S(2)}, u32[]{:S(2)}) collective-permute-start(f32[5,2,16,256]{3,2,1,0:T(8,128)S(1)} %get-tuple-element.42), channel_id=1, source_target_pairs={{4,0},{8,4},{12,8},{16,12},{20,16},{24,20},{28,24},{5,1},{9,5},{13... | collective-permute-start | bytes 491528 | tf_op jit(solution)/shard_map/ppermute | solution.py:22
  4.1 10.0 %collective-permute-start = (f32[5,2,16,256]{3,2,1,0:T(8,128)S(1)}, f32[5,2,16,256]{3,2,1,0:T(8,128)S(1)}, u32[]{:S(2)}, u32[]{:S(2)}) collective-permute-start(f32[5,2,16,256]{3,2,1,0:T(8,128)S(1)} %get-tuple-element.41), channel_id=1, source_target_pairs={{0,4},{4,8},{8,12},{12,16},{16,20},{20,24},{24,28},{1,5},{5,9},{9,... | collective-permute-start | bytes 491528 | tf_op jit(solution)/shard_map/ppermute | solution.py:21
  14.3 5.3 %collective-permute-start.3 = (f32[5,20,2,256]{3,2,1,0:T(2,128)S(1)}, f32[5,20,2,256]{3,2,1,0:T(2,128)S(1)}, u32[]{:S(2)}, u32[]{:S(2)}) collective-permute-start(f32[5,20,2,256]{3,2,1,0:T(2,128)S(1)} %get-tuple-element.36), channel_id=1, source_target_pairs={{1,0},{2,1},{3,2},{5,4},{6,5},{7,6},{9,8},{10,9},{11,10},{13,12},{... | collective-permute-start | bytes 614408 | tf_op jit(solution)/shard_map/ppermute | solution.py:22
  16.3 7.1 %collective-permute-start.2 = (f32[5,20,2,256]{3,2,1,0:T(2,128)S(1)}, f32[5,20,2,256]{3,2,1,0:T(2,128)S(1)}, u32[]{:S(2)}, u32[]{:S(2)}) collective-permute-start(f32[5,20,2,256]{3,2,1,0:T(2,128)S(1)} %get-tuple-element.35), channel_id=1, source_target_pairs={{0,1},{1,2},{2,3},{4,5},{5,6},{6,7},{8,9},{9,10},{10,11},{12,13},{... | collective-permute-start | bytes 614408 | tf_op jit(solution)/shard_map/ppermute | solution.py:21
  18.6 5.0 %copy-start.1 = (s32[16,16,256]{2,1,0:T(8,128)S(1)}, s32[16,16,256]{2,1,0:T(8,128)}, u32[]{:S(2)}) copy-start(s32[16,16,256]{2,1,0:T(8,128)} %param.11) | copy-start | bytes 786436
  18.7 5.0 %copy-start.2 = (f32[16,16,256]{2,1,0:T(8,128)S(1)}, f32[16,16,256]{2,1,0:T(8,128)}, u32[]{:S(2)}) copy-start(f32[16,16,256]{2,1,0:T(8,128)} %get-tuple-element.37) | copy-start | bytes 786436
  23.6 4.5 %copy-start.5 = (s32[48]{0:T(128)S(1)}, s32[48]{0:T(128)}, u32[]{:S(2)}) copy-start(s32[48]{0:T(128)} %param.12) | copy-start | bytes 580
  64.6 38.2 %copy-start.3 = (f32[16,6]{0,1:T(8,128)}, f32[16,6]{0,1:T(8,128)S(1)}, u32[]{:S(2)}) copy-start(f32[16,6]{0,1:T(8,128)S(1)} %fusion.103) | copy-start | bytes 1156
where the time goes:
time: 106 us; the launch traced here: 105 us
  blocking collectives  66.6 us (63%)
  local copies, waits for them, and re-layouts  11.2 us (11%)
  starting transfers between devices  10.2 us (10%)
  waiting for transfers between devices  8.72 us (8%)
  other arithmetic  6.48 us (6%)
  between operations  1.5 us (1%)
    unnamed x1, blocking collectives  36 us
    all_gather x1, blocking collectives, per_device(): slip_all = lax.all_gather(slip_own, 'strike', axis=1, tiled=True)  30.6 us
    ppermute x2, waiting for transfers between devices, with_halo(): before = lax.ppermute(last, axis, up)  7.27 us
    ppermute x2, starting transfers between devices, with_halo(): before = lax.ppermute(last, axis, up)  6.83 us
    another operation x4, other arithmetic, per_device(): return (jnp.stack([vx, vy, vz]), slip_own)  3.81 us
    ppermute x2, starting transfers between devices, with_halo(): after = lax.ppermute(first, axis, down)  3.36 us
    scatter x1, local copies, waits for them, and re-layouts, per_device(): vx.at[:, :, row - 1]  2.14 us
  transfers between devices with their start and end apart: 4, of which 4 were waited for; matrix products, arithmetic and copies ran while one was open for 1% of the time, Pallas kernels for 0%

commit v1 on v0

v1 whole, which is shorter than its diff:
```python
import functools

import jax
import jax.numpy as jnp
from jax import lax
from jax.experimental import pallas as pl
from jax.experimental.pallas import tpu as pltpu
from jax.sharding import PartitionSpec as P

NEWTON = 8
BUOY = (1.0, 0.8, 0.6, 1.25)
C_ONE = 9.0 / 8.0
C_TWO = -1.0 / 24.0
MESH = pl.DeviceIdType.MESH


def inverse_sinh(value):
    magnitude = jnp.log(jnp.abs(value) + jnp.sqrt(1.0 + value * value))
    return jnp.where(value < 0, -magnitude, magnitude)


def friction(tau_total, coef, psi, normal_stress):
    half_q = 0.5 * jnp.exp(psi / coef)
    scale = normal_stress * coef
    rate = jnp.zeros_like(tau_total)
    for _ in range(NEWTON):
        arg_val = rate * half_q
        resid = tau_total - rate - scale * inverse_sinh(arg_val)
        slope = -1.0 - scale * half_q / jnp.sqrt(1.0 + arg_val * arg_val)
        rate = rate - 0.35 * resid / slope
    return rate


def kernel(
    dims, vel, st, mat, po, fp, out, slip,
    sx, so, vb, mb, pb, ownp, zlo, zhi, packs, recv,
    lsem, psend, precv, xsend, xrecv, zsend, zrecv,
):
    n, nd, cx, cz, ny, fc, wide = dims
    row = ny // 2
    per = fc // n
    first_tile = n // 4
    tiles = fc // cx
    me = lax.axis_index("strike")
    dep = lax.axis_index("depth")

    loads = [
        pltpu.make_async_copy(st.at[0], sx.at[0, pl.ds(2, cx)], lsem.at[0]),
        pltpu.make_async_copy(st.at[3], sx.at[1, pl.ds(2, cx)], lsem.at[1]),
        pltpu.make_async_copy(fp, pb, lsem.at[2]),
        pltpu.make_async_copy(st.at[4], sx.at[2, pl.ds(2, cx)], lsem.at[3]),
        pltpu.make_async_copy(st.at[2], so.at[1], lsem.at[4]),
        pltpu.make_async_copy(st.at[5], so.at[2], lsem.at[5]),
        pltpu.make_async_copy(st.at[1], so.at[0], lsem.at[6]),
        pltpu.make_async_copy(mat, mb, lsem.at[7]),
        pltpu.make_async_copy(vel, vb, lsem.at[8]),
    ]
    for load in loads:
        load.start()

    has_left, has_right = me > 0, me < n - 1
    has_below, has_above = dep > 0, dep < nd - 1
    barrier = pltpu.get_barrier_semaphore()
    for k in range(1, n):
        peer = lax.rem(me + k, n)
        pl.semaphore_signal(barrier, inc=1, device_id=(peer, dep), device_id_type=MESH)

    @pl.when(has_below)
    def _():
        pl.semaphore_signal(barrier, inc=1, device_id=(me, dep - 1), device_id_type=MESH)

    @pl.when(has_above)
    def _():
        pl.semaphore_signal(barrier, inc=1, device_id=(me, dep + 1), device_id_type=MESH)

    zero_row = jnp.zeros((2, cz, ny), jnp.float32)

    @pl.when(jnp.logical_not(has_left))
    def _():
        for f in range(3):
            sx[f, 0:2] = zero_row

    @pl.when(jnp.logical_not(has_right))
    def _():
        for f in range(3):
            sx[f, cx + 2 : cx + 4] = zero_row

    @pl.when(jnp.logical_not(has_below))
    def _():
        zlo[...] = jnp.zeros(zlo.shape, jnp.float32)

    @pl.when(jnp.logical_not(has_above))
    def _():
        zhi[...] = jnp.zeros(zhi.shape, jnp.float32)

    lane = lax.broadcasted_iota(jnp.int32, (cz, wide), 1)
    lane_one = lax.broadcasted_iota(jnp.int32, (cz, 128), 1)
    loads[0].wait()
    loads[1].wait()
    loads[2].wait()
    near = jnp.logical_and(me >= first_tile - 1, me <= first_tile + tiles)
    base = jnp.where(near, 4 * cx + (me - first_tile) * cx, -4 * wide)
    normal = jnp.zeros((cz, wide), jnp.float32)
    shear = jnp.zeros((cz, wide), jnp.float32)
    for i in range(cx):
        here = lane == base + i
        normal = jnp.where(here, sx[0, 2 + i, :, row : row + 1], normal)
        shear = jnp.where(here, sx[1, 2 + i, :, row : row + 1], shear)
    dxx = C_ONE * (normal - pltpu.roll(normal, 1, 1)) + C_TWO * (
        pltpu.roll(normal, wide - 1, 1) - pltpu.roll(normal, 2, 1)
    )
    share = shear + 0.5 * dxx
    share = jnp.where(jnp.logical_and(lane >= 4 * cx, lane < 4 * cx + fc), share, 0.0)
    blocks = [share for _ in range(tiles)]
    for f in range(4):
        mine = jnp.full((cz, 128), 1.0, jnp.float32)
        for j in range(per):
            column = po[me * per + j]
            value = pb[f, :, j : j + 1]
            mine = jnp.where(lane_one == cx + j, value, mine)
            for t in range(tiles):
                local = column - t * cx
                held = jnp.logical_and(local >= 0, local < cx)
                place = jnp.where(held, f * cx + local, -1)
                blocks[t] = jnp.where(lane == place, value, blocks[t])
        ownp[f] = mine
    for t in range(tiles):
        packs[t] = blocks[t]
    my_tile = jnp.clip(me - first_tile, 0, tiles - 1)
    recv[me] = packs[my_tile]

    for load in loads[3:6]:
        load.wait()
    pl.semaphore_wait(
        barrier, n - 1 + has_below.astype(jnp.int32) + has_above.astype(jnp.int32)
    )

    def pack_copy(k):
        peer = lax.rem(me + k, n)
        return pltpu.make_async_remote_copy(
            src_ref=packs.at[jnp.clip(peer - first_tile, 0, tiles - 1)],
            dst_ref=recv.at[me],
            send_sem=psend.at[k],
            recv_sem=precv.at[me],
            device_id=(peer, dep),
            device_id_type=MESH,
        )

    def pack_arrival(k):
        source = lax.rem(me + k, n)
        return pltpu.make_async_remote_copy(
            src_ref=packs.at[0],
            dst_ref=recv.at[source],
            send_sem=psend.at[k],
            recv_sem=precv.at[source],
            device_id=(source, dep),
            device_id_type=MESH,
        )

    def x_copy(f, up):
        if up:
            rows = 2 if f == 0 else 1
            src, dst, to = cx + 2 - rows, 2 - rows, me + 1
        else:
            rows = 1 if f == 0 else 2
            src, dst, to = 2, cx + 2, me - 1
        slot = f if up else 3 + f
        return pltpu.make_async_remote_copy(
            src_ref=sx.at[f, pl.ds(src, rows)],
            dst_ref=sx.at[f, pl.ds(dst, rows)],
            send_sem=xsend.at[slot],
            recv_sem=xrecv.at[slot],
            device_id=(to, dep),
            device_id_type=MESH,
        )

    def z_copy(f, up):
        field = (sx.at[2, pl.ds(2, cx)], so.at[2], so.at[1])[f]
        if up:
            rows = 1 if f == 2 else 2
            src, dst, to = cz - rows, zlo.at[f, :, pl.ds(8 - rows, rows)], dep + 1
        else:
            rows = 2 if f == 2 else 1
            src, dst, to = 0, zhi.at[f, :, pl.ds(0, rows)], dep - 1
        slot = f if up else 3 + f
        return pltpu.make_async_remote_copy(
            src_ref=field.at[:, pl.ds(src, rows)],
            dst_ref=dst,
            send_sem=zsend.at[slot],
            recv_sem=zrecv.at[slot],
            device_id=(me, to),
            device_id_type=MESH,
        )

    for k in range(1, n):
        pack_copy(k).start()

    @pl.when(has_above)
    def _():
        for f in range(3):
            z_copy(f, True).start()

    @pl.when(has_below)
    def _():
        for f in range(3):
            z_copy(f, False).start()

    @pl.when(has_right)
    def _():
        for f in range(3):
            x_copy(f, True).start()

    @pl.when(has_left)
    def _():
        for f in range(3):
            x_copy(f, False).start()

    for load in loads[6:]:
        load.wait()

    @pl.when(has_below)
    def _():
        for f in range(3):
            z_copy(f, True).wait_recv()

    @pl.when(has_above)
    def _():
        for f in range(3):
            z_copy(f, False).wait_recv()

    yi = lax.broadcasted_iota(jnp.int32, (cz, ny), 1)

    def y_at(field, offset):
        moved = pltpu.roll(field, (-offset) % ny, 1)
        keep = yi < ny - offset if offset > 0 else yi >= -offset
        return jnp.where(keep, moved, 0.0)

    def z_at(f, field, x):
        joined = jnp.concatenate([zlo[f, x], field, zhi[f, x]], axis=0)
        total = cz + 16
        return lambda offset: pltpu.roll(joined, (-offset) % total, 0)[8 : 8 + cz]

    def minus(at):
        return C_ONE * (at(0) - at(-1)) + C_TWO * (at(1) - at(-2))

    def plus(at):
        return C_ONE * (at(1) - at(0)) + C_TWO * (at(2) - at(-1))

    def along_x(f, x):
        return lambda offset: sx[f, x + 2 + offset]

    def along_y(field):
        return lambda offset: field if offset == 0 else y_at(field, offset)

    def plane(x):
        material = mb[x]
        b = jnp.zeros((cz, ny), jnp.float32)
        for index in range(4):
            b = jnp.where(material == index, BUOY[index], b)
        b = 0.25 * b
        sxy, sxz = sx[1, x + 2], sx[2, x + 2]
        syy, szz, syz = so[0, x], so[1, x], so[2, x]
        out[0, x] = vb[0, x] + b * (
            minus(along_x(0, x)) + minus(along_y(sxy)) + minus(z_at(0, sxz, x))
        )
        out[1, x] = vb[1, x] + b * (
            plus(along_x(1, x)) + plus(along_y(syy)) + minus(z_at(1, syz, x))
        )
        out[2, x] = vb[2, x] + b * (
            plus(along_x(2, x)) + plus(along_y(syz)) + plus(z_at(2, szz, x))
        )

    def step(x, carry):
        plane(x)
        return carry

    lax.fori_loop(2, cx - 2, step, 0)

    for k in range(1, n):
        pack_arrival(k).wait_recv()
    total = recv[0]
    for k in range(1, n):
        total = total + recv[k]
    used = lane_one < cx
    fields = []
    for f in range(4):
        moved = total if f == 0 else pltpu.roll(total, wide - f * cx, 1)
        fields.append(jnp.where(used, moved[:, :128], ownp[f]))
    tau = jnp.zeros((cz, 128), jnp.float32)
    for t in range(tiles):
        moved = pltpu.roll(total, wide - (4 + t) * cx, 1)[:, :128]
        tau = jnp.where(jnp.logical_and(used, my_tile == t), moved, tau)
    for j in range(per):
        picked = jnp.where(lane == 4 * cx + po[me * per + j], total, 0.0)
        tau = jnp.where(lane_one == cx + j, jnp.sum(picked, axis=1, keepdims=True), tau)
    rate = friction(tau + fields[3], fields[0], fields[1], fields[2])
    slip[...] = pltpu.roll(rate, 128 - cx, 1)[:, :per]

    @pl.when(has_left)
    def _():
        for f in range(3):
            x_copy(f, True).wait_recv()

    @pl.when(has_right)
    def _():
        for f in range(3):
            x_copy(f, False).wait_recv()

    def edge(i, carry):
        plane(i + (cx - 4) * (i // 2))
        return carry

    lax.fori_loop(0, 4, edge, 0)

    @pl.when(jnp.logical_and(me >= first_tile, me < first_tile + tiles))
    def _():
        for i in range(cx):
            s = 0.5 * rate[:, i : i + 1]
            low = out[0, i, :, row - 128 : row]
            high = out[0, i, :, row : row + 128]
            middle = 0.5 * (high + pltpu.roll(low, 1, 1))
            out[0, i, :, row : row + 128] = jnp.where(lane_one == 0, middle + s, high)
            out[0, i, :, row - 128 : row] = jnp.where(
                lane_one == 127, pltpu.roll(middle, 127, 1) - s, low
            )

    for k in range(1, n):
        pack_copy(k).wait_send()

    @pl.when(has_above)
    def _():
        for f in range(3):
            z_copy(f, True).wait_send()

    @pl.when(has_below)
    def _():
        for f in range(3):
            z_copy(f, False).wait_send()

    @pl.when(has_right)
    def _():
        for f in range(3):
            x_copy(f, True).wait_send()

    @pl.when(has_left)
    def _():
        for f in range(3):
            x_copy(f, False).wait_send()


def per_device(n, nd, velocity, stress, material, patch_order, fault_params):
    _, cx, cz, ny = stress.shape
    fc = patch_order.shape[0]
    per = fc // n
    wide = -(-(4 * cx + fc + 2) // 128) * 128
    dims = (n, nd, cx, cz, ny, fc, wide)
    tiles = fc // cx
    f32 = jnp.float32
    anywhere = pl.BlockSpec(memory_space=pl.ANY)
    dma = pltpu.SemaphoreType.DMA
    return pl.pallas_call(
        functools.partial(kernel, dims),
        out_shape=(
            jax.ShapeDtypeStruct(velocity.shape, f32),
            jax.ShapeDtypeStruct((cz, per), f32),
        ),
        in_specs=[anywhere, anywhere, anywhere, pl.BlockSpec(memory_space=pltpu.SMEM), anywhere],
        out_specs=(pl.BlockSpec(memory_space=pltpu.VMEM), pl.BlockSpec(memory_space=pltpu.VMEM)),
        scratch_shapes=[
            pltpu.VMEM((3, cx + 4, cz, ny), f32),
            pltpu.VMEM((3, cx, cz, ny), f32),
            pltpu.VMEM((3, cx, cz, ny), f32),
            pltpu.VMEM((cx, cz, ny), jnp.int32),
            pltpu.VMEM((4, cz, per), f32),
            pltpu.VMEM((4, cz, 128), f32),
            pltpu.VMEM((3, cx, 8, ny), f32),
            pltpu.VMEM((3, cx, 8, ny), f32),
            pltpu.VMEM((tiles, cz, wide), f32),
            pltpu.VMEM((n, cz, wide), f32),
            dma((9,)),
            dma((n,)),
            dma((n,)),
            dma((6,)),
            dma((6,)),
            dma((6,)),
            dma((6,)),
        ],
        compiler_params=pltpu.CompilerParams(collective_id=0, has_side_effects=True),
    )(velocity, stress, material, patch_order, fault_params)


def solution(mesh):
    n, nd = mesh.shape["strike"], mesh.shape["depth"]
    return jax.shard_map(
        functools.partial(per_device, n, nd),
        mesh=mesh,
        in_specs=(
            P(None, "strike", "depth", None),
            P(None, "strike", "depth", None),
            P("strike", "depth", None),
            P(),
            P(None, "depth", "strike"),
        ),
        out_specs=(P(None, "strike", "depth", None), P("depth", "strike")),
        check_vma=False,
    )
```

time: 106 us -> 19.2 us (0.18)
  the two profiles are of different devices: /device:TPU:2 before, /device:TPU:1 now
where the time goes in v1:
time: 19.2 us; the launch traced here: 18.9 us
  Pallas kernels  13.5 us (70%)
  local copies, waits for them, and re-layouts  4.84 us (25%)
  between operations  0.64 us (3%)
    pallas_call x1, Pallas kernels, per_device(): pl.pallas_call(functools.partial(kernel, dims), out_shape=(jax.ShapeDtype...  13.5 us
    unnamed x2, local copies, waits for them, and re-layouts  3.48 us
    pallas_call x1, local copies, waits for them, and re-layouts, per_device(): pl.pallas_call(functools.partial(kernel, dims), out_shape=(jax.ShapeDtype...  1.36 us

profile of v1, /device:TPU:1, one launch (start us, length us, event | category | flops | bytes accessed | tf_op | source)
XLA Modules:
  0.0 18.9 jit_solution(15191796778174374347)
XLA Ops:
  0.6 1.4 %copy.7.fp = f32[4,16,6]{2,1,0:T(8,128)} copy(f32[4,16,6]{1,0,2:T(4,128)} %param.9) | data formatting | bytes 3072 | tf_op args[4]
  2.0 13.5 %shard_map.68 = (f32[3,16,16,256]{3,2,1,0:T(8,128)}, f32[16,6]{1,0:T(8,128)}) custom-call(f32[3,16,16,256]{3,2,1,0:T(8,128)} %vel.1, f32[6,16,16,256]{3,2,1,0:T(8,128)} %st.1, s32[16,16,256]{2,1,0:T(8,128)} %mat.1, s32[48]{0:T(128)} %po.1, f32[4,16,6]{2,1,0:T(8,128)} %copy.7.fp), custom_call_target="tpu_custom_call" | custom-call | tf_op jit(solution)/shard_map/pallas_call | solution.py:361
  15.5 1.4 %copy.8 = f32[16,6]{0,1:T(8,128)} copy(f32[16,6]{1,0:T(8,128)} %get-tuple-element.3) | data formatting | bytes 768 | tf_op jit(solution)/shard_map/pallas_call | solution.py:361
  16.9 2.1 %copy.10 = f32[3,16,16,256]{3,2,1,0:T(8,128)} copy(f32[3,16,16,256]{3,2,1,0:T(8,128)} %get-tuple-element.6) | data formatting | bytes 1572864

commit v2 on v1

--- a/solution.py
+++ b/solution.py
@@ -112,11 +112,12 @@
     share = shear + 0.5 * dxx
     share = jnp.where(jnp.logical_and(lane >= 4 * cx, lane < 4 * cx + fc), share, 0.0)
     blocks = [share for _ in range(tiles)]
+    params = [pb[j].T for j in range(per)]
     for f in range(4):
         mine = jnp.full((cz, 128), 1.0, jnp.float32)
         for j in range(per):
             column = po[me * per + j]
-            value = pb[f, :, j : j + 1]
+            value = params[j][:, f : f + 1]
             mine = jnp.where(lane_one == cx + j, value, mine)
             for t in range(tiles):
                 local = column - t * cx
@@ -294,7 +295,7 @@
         picked = jnp.where(lane == 4 * cx + po[me * per + j], total, 0.0)
         tau = jnp.where(lane_one == cx + j, jnp.sum(picked, axis=1, keepdims=True), tau)
     rate = friction(tau + fields[3], fields[0], fields[1], fields[2])
-    slip[...] = pltpu.roll(rate, 128 - cx, 1)[:, :per]
+    slip[...] = rate.T[cx : cx + per]
 
     @pl.when(has_left)
     def _():
@@ -348,6 +349,15 @@
             x_copy(f, False).wait_send()
 
 
+def write_out(held, slip, out, slip_out, sem):
+    copies = [pltpu.make_async_copy(slip, slip_out, sem.at[3])]
+    copies += [pltpu.make_async_copy(held.at[c], out.at[c], sem.at[c]) for c in range(3)]
+    for copy in copies:
+        copy.start()
+    for copy in copies:
+        copy.wait()
+
+
 def per_device(n, nd, velocity, stress, material, patch_order, fault_params):
     _, cx, cz, ny = stress.shape
     fc = patch_order.shape[0]
@@ -356,13 +366,13 @@
     dims = (n, nd, cx, cz, ny, fc, wide)
     tiles = fc // cx
     f32 = jnp.float32
-    anywhere = pl.BlockSpec(memory_space=pl.ANY)
+    anywhere = pl.BlockSpec(memory_space=pltpu.HBM)
     dma = pltpu.SemaphoreType.DMA
-    return pl.pallas_call(
+    held = pl.pallas_call(
         functools.partial(kernel, dims),
         out_shape=(
             jax.ShapeDtypeStruct(velocity.shape, f32),
-            jax.ShapeDtypeStruct((cz, per), f32),
+            jax.ShapeDtypeStruct((per, cz), f32),
         ),
         in_specs=[anywhere, anywhere, anywhere, pl.BlockSpec(memory_space=pltpu.SMEM), anywhere],
         out_specs=(pl.BlockSpec(memory_space=pltpu.VMEM), pl.BlockSpec(memory_space=pltpu.VMEM)),
@@ -371,7 +381,7 @@
             pltpu.VMEM((3, cx, cz, ny), f32),
             pltpu.VMEM((3, cx, cz, ny), f32),
             pltpu.VMEM((cx, cz, ny), jnp.int32),
-            pltpu.VMEM((4, cz, per), f32),
+            pltpu.VMEM((per, 4, cz), f32),
             pltpu.VMEM((4, cz, 128), f32),
             pltpu.VMEM((3, cx, 8, ny), f32),
             pltpu.VMEM((3, cx, 8, ny), f32),
@@ -385,8 +395,21 @@
             dma((6,)),
             dma((6,)),
         ],
-        compiler_params=pltpu.CompilerParams(collective_id=0, has_side_effects=True),
-    )(velocity, stress, material, patch_order, fault_params)
+        compiler_params=pltpu.CompilerParams(collective_id=0, has_side_effects=True, vmem_limit_bytes=12 << 20),
+    )(velocity, stress, material, patch_order, jnp.transpose(fault_params, (2, 0, 1)))
+    resident = pl.BlockSpec(memory_space=pltpu.VMEM)
+    moved, slip = pl.pallas_call(
+        write_out,
+        out_shape=(
+            jax.ShapeDtypeStruct(velocity.shape, f32),
+            jax.ShapeDtypeStruct((per, cz), f32),
+        ),
+        in_specs=[resident, resident],
+        out_specs=(anywhere, anywhere),
+        scratch_shapes=[dma((4,))],
+        compiler_params=pltpu.CompilerParams(vmem_limit_bytes=4 << 20),
+    )(*held)
+    return moved, slip.T
 
 
 def solution(mesh):

time: 19.2 us -> 19.4 us (1.010)
    unnamed x2 -> x10, local copies, waits for them, and re-layouts: 3.48 us -> 4.84 us
    pallas_call x1 -> x0, local copies, waits for them, and re-layouts: 1.36 us -> none  [per_device(): pl.pallas_call(functools.partial(kernel, dims), out_shape=(jax.ShapeDtype...]
    pallas_call x0 -> x1, Pallas kernels: none -> 0.92 us  [per_device(): pl.pallas_call(write_out, out_shape=(jax.ShapeDtypeStruct(velocity.shape,...]
    pallas_call x1, Pallas kernels: 13.5 us -> 12.7 us  [per_device(): pl.pallas_call(functools.partial(kernel, dims), out_shape=(jax.ShapeDtype...]
where the time goes in v2:
time: 19.4 us; the launch traced here: 19.1 us
  Pallas kernels  13.6 us (70%)
  local copies, waits for them, and re-layouts  4.84 us (25%)
  between operations  0.65 us (3%)
    pallas_call x1, Pallas kernels, per_device(): pl.pallas_call(functools.partial(kernel, dims), out_shape=(jax.ShapeDtype...  12.7 us
    unnamed x10, local copies, waits for them, and re-layouts  4.84 us
    pallas_call x1, Pallas kernels, per_device(): pl.pallas_call(write_out, out_shape=(jax.ShapeDtypeStruct(velocity.shape,...  0.92 us

profile of v2, /device:TPU:1, one launch (start us, length us, event | category | flops | bytes accessed | tf_op | source)
XLA Modules:
  0.0 19.1 jit_solution(10983572829940978580)
XLA Ops:
  0.6 0.0 copy-start
  0.6 1.4 %copy-done = f32[6,16,16,256]{3,2,1,0:T(8,128)S(1)} copy-done((f32[6,16,16,256]{3,2,1,0:T(8,128)S(1)}, f32[6,16,16,256]{3,2,1,0:T(8,128)}, u32[]{:S(2)}) %copy-start) | copy-done | bytes 1572888
  2.0 0.0 copy-start.1
  2.0 1.1 %copy-done.1 = f32[3,16,16,256]{3,2,1,0:T(8,128)S(1)} copy-done((f32[3,16,16,256]{3,2,1,0:T(8,128)S(1)}, f32[3,16,16,256]{3,2,1,0:T(8,128)}, u32[]{:S(2)}) %copy-start.1) | copy-done | bytes 786456
  3.2 0.0 copy-start.2
  3.2 0.9 %copy-done.2 = s32[16,16,256]{2,1,0:T(8,128)S(1)} copy-done((s32[16,16,256]{2,1,0:T(8,128)S(1)}, s32[16,16,256]{2,1,0:T(8,128)}, u32[]{:S(2)}) %copy-start.2) | copy-done | bytes 262168
  4.1 0.0 copy-start.3
  4.1 0.7 %copy-done.3 = f32[4,16,6]{1,0,2:T(4,128)S(1)} copy-done((f32[4,16,6]{1,0,2:T(4,128)S(1)}, f32[4,16,6]{1,0,2:T(4,128)}, u32[]{:S(2)}) %copy-start.3) | copy-done | bytes 1560
  4.8 0.0 copy-start.4
  4.8 0.7 %copy-done.4 = s32[48]{0:T(128)S(1)} copy-done((s32[48]{0:T(128)S(1)}, s32[48]{0:T(128)}, u32[]{:S(2)}) %copy-start.4) | copy-done | bytes 216
  5.5 12.7 %shard_map.68 = (f32[3,16,16,256]{3,2,1,0:T(8,128)S(1)}, f32[6,16]{1,0:T(8,128)S(1)}) custom-call(f32[3,16,16,256]{3,2,1,0:T(8,128)S(1)} %copy-done.1, f32[6,16,16,256]{3,2,1,0:T(8,128)S(1)} %copy-done, s32[16,16,256]{2,1,0:T(8,128)S(1)} %copy-done.2, s32[48]{0:T(128)S(1)} %copy-done.4, f32[6,4,16]{2,1,0:T(4,128)S(1)} %bitcast.2), custom_call_target="tpu_custom_call" | custom-call | tf_op jit(solution)/shard_map/pallas_call | solution.py:371
  18.2 0.9 %shard_map.69 = (f32[3,16,16,256]{3,2,1,0:T(8,128)}, f32[6,16]{1,0:T(8,128)}) custom-call(f32[3,16,16,256]{3,2,1,0:T(8,128)S(1)} %get-tuple-element.6.held, f32[6,16]{1,0:T(8,128)S(1)} %get-tuple-element.7.slip), custom_call_target="tpu_custom_call" | custom-call | tf_op jit(solution)/shard_map/pallas_call | solution.py:401
Async XLA Ops:
  0.6 1.4 %copy-start = (f32[6,16,16,256]{3,2,1,0:T(8,128)S(1)}, f32[6,16,16,256]{3,2,1,0:T(8,128)}, u32[]{:S(2)}) copy-start(f32[6,16,16,256]{3,2,1,0:T(8,128)} %st.1) | copy-start | bytes 4718596
  2.0 1.1 %copy-start.1 = (f32[3,16,16,256]{3,2,1,0:T(8,128)S(1)}, f32[3,16,16,256]{3,2,1,0:T(8,128)}, u32[]{:S(2)}) copy-start(f32[3,16,16,256]{3,2,1,0:T(8,128)} %vel.1) | copy-start | bytes 2359300
  3.2 0.9 %copy-start.2 = (s32[16,16,256]{2,1,0:T(8,128)S(1)}, s32[16,16,256]{2,1,0:T(8,128)}, u32[]{:S(2)}) copy-start(s32[16,16,256]{2,1,0:T(8,128)} %mat.1) | copy-start | bytes 786436
  4.1 0.7 %copy-start.3 = (f32[4,16,6]{1,0,2:T(4,128)S(1)}, f32[4,16,6]{1,0,2:T(4,128)}, u32[]{:S(2)}) copy-start(f32[4,16,6]{1,0,2:T(4,128)} %param.9) | copy-start | bytes 4612
  4.8 0.7 %copy-start.4 = (s32[48]{0:T(128)S(1)}, s32[48]{0:T(128)}, u32[]{:S(2)}) copy-start(s32[48]{0:T(128)} %po.1) | copy-start | bytes 580

commit v3 on v2

--- a/solution.py
+++ b/solution.py
@@ -32,8 +32,8 @@
 
 
 def kernel(
-    dims, vel, st, mat, po, fp, out, slip,
-    sx, so, vb, mb, pb, ownp, zlo, zhi, packs, recv,
+    dims, vel, st, mat, order, fp, out, slip,
+    po, sx, so, vb, mb, pb, ownp, zlo, zhi, packs, recv,
     lsem, psend, precv, xsend, xrecv, zsend, zrecv,
 ):
     n, nd, cx, cz, ny, fc, wide = dims
@@ -54,8 +54,9 @@
         pltpu.make_async_copy(st.at[1], so.at[0], lsem.at[6]),
         pltpu.make_async_copy(mat, mb, lsem.at[7]),
         pltpu.make_async_copy(vel, vb, lsem.at[8]),
+        pltpu.make_async_copy(order, po, lsem.at[9]),
     ]
-    for load in loads:
+    for load in loads[9:] + loads[:9]:
         load.start()
 
     has_left, has_right = me > 0, me < n - 1
@@ -98,6 +99,7 @@
     loads[0].wait()
     loads[1].wait()
     loads[2].wait()
+    loads[9].wait()
     near = jnp.logical_and(me >= first_tile - 1, me <= first_tile + tiles)
     base = jnp.where(near, 4 * cx + (me - first_tile) * cx, -4 * wide)
     normal = jnp.zeros((cz, wide), jnp.float32)
@@ -216,7 +218,7 @@
         for f in range(3):
             x_copy(f, False).start()
 
-    for load in loads[6:]:
+    for load in loads[6:9]:
         load.wait()
 
     @pl.when(has_below)
@@ -368,15 +370,18 @@
     f32 = jnp.float32
     anywhere = pl.BlockSpec(memory_space=pltpu.HBM)
     dma = pltpu.SemaphoreType.DMA
+    params = jnp.transpose(fault_params, (2, 0, 1))
+    big = (velocity, stress, material, patch_order, params)
     held = pl.pallas_call(
         functools.partial(kernel, dims),
         out_shape=(
             jax.ShapeDtypeStruct(velocity.shape, f32),
             jax.ShapeDtypeStruct((per, cz), f32),
         ),
-        in_specs=[anywhere, anywhere, anywhere, pl.BlockSpec(memory_space=pltpu.SMEM), anywhere],
+        in_specs=[anywhere] * 5,
         out_specs=(pl.BlockSpec(memory_space=pltpu.VMEM), pl.BlockSpec(memory_space=pltpu.VMEM)),
         scratch_shapes=[
+            pltpu.SMEM((fc,), jnp.int32),
             pltpu.VMEM((3, cx + 4, cz, ny), f32),
             pltpu.VMEM((3, cx, cz, ny), f32),
             pltpu.VMEM((3, cx, cz, ny), f32),
@@ -387,7 +392,7 @@
             pltpu.VMEM((3, cx, 8, ny), f32),
             pltpu.VMEM((tiles, cz, wide), f32),
             pltpu.VMEM((n, cz, wide), f32),
-            dma((9,)),
+            dma((10,)),
             dma((n,)),
             dma((n,)),
             dma((6,)),
@@ -396,7 +401,7 @@
             dma((6,)),
         ],
         compiler_params=pltpu.CompilerParams(collective_id=0, has_side_effects=True, vmem_limit_bytes=12 << 20),
-    )(velocity, stress, material, patch_order, jnp.transpose(fault_params, (2, 0, 1)))
+    )(*[pltpu.with_memory_space_constraint(v, pltpu.HBM) for v in big])
     resident = pl.BlockSpec(memory_space=pltpu.VMEM)
     moved, slip = pl.pallas_call(
         write_out,

time: 19.4 us -> 13.7 us (0.71)
  local copies, waits for them, and re-layouts: 4.84 us -> 0 us
  Pallas kernels: 13.6 us -> 12.9 us
    unnamed x10 -> x0, local copies, waits for them, and re-layouts: 4.84 us -> none
    pallas_call x1, Pallas kernels: 12.7 us -> 11.9 us  [per_device(): pl.pallas_call(functools.partial(kernel, dims), out_shape=(jax.ShapeDtype...]
where the time goes in v3:
time: 13.7 us; the launch traced here: 13.5 us
  Pallas kernels  12.9 us (94%)
  between operations  0.64 us (5%)
    pallas_call x1, Pallas kernels, per_device(): pl.pallas_call(functools.partial(kernel, dims), out_shape=(jax.ShapeDtype...  11.9 us
    pallas_call x1, Pallas kernels, per_device(): pl.pallas_call(write_out, out_shape=(jax.ShapeDtypeStruct(velocity.shape,...  0.92 us

profile of v3, /device:TPU:1, one launch (start us, length us, event | category | flops | bytes accessed | tf_op | source)
XLA Modules:
  0.0 13.5 jit_solution(16685227779268138267)
XLA Ops:
  0.6 11.9 %shard_map.68 = (f32[3,16,16,256]{3,2,1,0:T(8,128)S(1)}, f32[6,16]{1,0:T(8,128)S(1)}) custom-call(f32[3,16,16,256]{3,2,1,0:T(8,128)} %vel.1, f32[6,16,16,256]{3,2,1,0:T(8,128)} %st.1, s32[16,16,256]{2,1,0:T(8,128)} %mat.1, s32[48]{0:T(128)} %order.1, f32[6,4,16]{2,1,0:T(4,128)} %bitcast.2), custom_call_target="tpu_custom_call" | custom-call | tf_op jit(solution)/shard_map/pallas_call | solution.py:375
  12.6 0.9 %shard_map.69 = (f32[3,16,16,256]{3,2,1,0:T(8,128)}, f32[6,16]{1,0:T(8,128)}) custom-call(f32[3,16,16,256]{3,2,1,0:T(8,128)S(1)} %get-tuple-element.6.held, f32[6,16]{1,0:T(8,128)S(1)} %get-tuple-element.7.slip), custom_call_target="tpu_custom_call" | custom-call | tf_op jit(solution)/shard_map/pallas_call | solution.py:406

commit v4 on v3

--- a/solution.py
+++ b/solution.py
@@ -14,20 +14,17 @@
 MESH = pl.DeviceIdType.MESH
 
 
-def inverse_sinh(value):
-    magnitude = jnp.log(jnp.abs(value) + jnp.sqrt(1.0 + value * value))
-    return jnp.where(value < 0, -magnitude, magnitude)
-
-
 def friction(tau_total, coef, psi, normal_stress):
     half_q = 0.5 * jnp.exp(psi / coef)
     scale = normal_stress * coef
+    stiff = scale * half_q
     rate = jnp.zeros_like(tau_total)
     for _ in range(NEWTON):
         arg_val = rate * half_q
-        resid = tau_total - rate - scale * inverse_sinh(arg_val)
-        slope = -1.0 - scale * half_q / jnp.sqrt(1.0 + arg_val * arg_val)
-        rate = rate - 0.35 * resid / slope
+        root = jnp.sqrt(1.0 + arg_val * arg_val)
+        magnitude = jnp.log(jnp.abs(arg_val) + root)
+        resid = tau_total - rate - scale * jnp.where(arg_val < 0, -magnitude, magnitude)
+        rate = rate + 0.35 * resid * (root / (root + stiff))
     return rate
 
 
@@ -56,9 +53,6 @@
         pltpu.make_async_copy(vel, vb, lsem.at[8]),
         pltpu.make_async_copy(order, po, lsem.at[9]),
     ]
-    for load in loads[9:] + loads[:9]:
-        load.start()
-
     has_left, has_right = me > 0, me < n - 1
     has_below, has_above = dep > 0, dep < nd - 1
     barrier = pltpu.get_barrier_semaphore()
@@ -73,6 +67,9 @@
     @pl.when(has_above)
     def _():
         pl.semaphore_signal(barrier, inc=1, device_id=(me, dep + 1), device_id_type=MESH)
+
+    for load in loads[9:] + loads[:9]:
+        load.start()
 
     zero_row = jnp.zeros((2, cz, ny), jnp.float32)
 
@@ -221,16 +218,6 @@
     for load in loads[6:9]:
         load.wait()
 
-    @pl.when(has_below)
-    def _():
-        for f in range(3):
-            z_copy(f, True).wait_recv()
-
-    @pl.when(has_above)
-    def _():
-        for f in range(3):
-            z_copy(f, False).wait_recv()
-
     yi = lax.broadcasted_iota(jnp.int32, (cz, ny), 1)
 
     def y_at(field, offset):
@@ -238,8 +225,11 @@
         keep = yi < ny - offset if offset > 0 else yi >= -offset
         return jnp.where(keep, moved, 0.0)
 
-    def z_at(f, field, x):
-        joined = jnp.concatenate([zlo[f, x], field, zhi[f, x]], axis=0)
+    blank = jnp.zeros((8, ny), jnp.float32)
+
+    def z_at(f, field, x, faces):
+        ends = (zlo[f, x], zhi[f, x]) if faces else (blank, blank)
+        joined = jnp.concatenate([ends[0], field, ends[1]], axis=0)
         total = cz + 16
         return lambda offset: pltpu.roll(joined, (-offset) % total, 0)[8 : 8 + cz]
 
@@ -255,29 +245,52 @@
     def along_y(field):
         return lambda offset: field if offset == 0 else y_at(field, offset)
 
-    def plane(x):
+    def buoyancy(x):
         material = mb[x]
         b = jnp.zeros((cz, ny), jnp.float32)
         for index in range(4):
             b = jnp.where(material == index, BUOY[index], b)
-        b = 0.25 * b
+        return 0.25 * b
+
+    def plane(x, faces):
+        b = buoyancy(x)
         sxy, sxz = sx[1, x + 2], sx[2, x + 2]
         syy, szz, syz = so[0, x], so[1, x], so[2, x]
         out[0, x] = vb[0, x] + b * (
-            minus(along_x(0, x)) + minus(along_y(sxy)) + minus(z_at(0, sxz, x))
+            minus(along_x(0, x)) + minus(along_y(sxy)) + minus(z_at(0, sxz, x, faces))
         )
         out[1, x] = vb[1, x] + b * (
-            plus(along_x(1, x)) + plus(along_y(syy)) + minus(z_at(1, syz, x))
+            plus(along_x(1, x)) + plus(along_y(syy)) + minus(z_at(1, syz, x, faces))
         )
         out[2, x] = vb[2, x] + b * (
-            plus(along_x(2, x)) + plus(along_y(syz)) + plus(z_at(2, szz, x))
+            plus(along_x(2, x)) + plus(along_y(syz)) + plus(z_at(2, szz, x, faces))
         )
 
     def step(x, carry):
-        plane(x)
+        plane(x, False)
         return carry
 
     lax.fori_loop(2, cx - 2, step, 0)
+
+    @pl.when(has_below)
+    def _():
+        for f in range(3):
+            z_copy(f, True).wait_recv()
+
+    @pl.when(has_above)
+    def _():
+        for f in range(3):
+            z_copy(f, False).wait_recv()
+
+    def face(x, carry):
+        b = buoyancy(x)
+        nothing = jnp.zeros((cz, ny), jnp.float32)
+        out[0, x] += b * minus(z_at(0, nothing, x, True))
+        out[1, x] += b * minus(z_at(1, nothing, x, True))
+        out[2, x] += b * plus(z_at(2, nothing, x, True))
+        return carry
+
+    lax.fori_loop(2, cx - 2, face, 0)
 
     for k in range(1, n):
         pack_arrival(k).wait_recv()
@@ -310,7 +323,7 @@
             x_copy(f, False).wait_recv()
 
     def edge(i, carry):
-        plane(i + (cx - 4) * (i // 2))
+        plane(i + (cx - 4) * (i // 2), True)
         return carry
 
     lax.fori_loop(0, 4, edge, 0)

time: 13.7 us -> 12.5 us (0.912)
  Pallas kernels: 12.9 us -> 11.7 us
    pallas_call x1, Pallas kernels: 11.9 us -> 10.8 us  [per_device(): pl.pallas_call(functools.partial(kernel, dims), out_shape=(jax.ShapeDtype...]
where the time goes in v4:
time: 12.5 us; the launch traced here: 12.4 us
  Pallas kernels  11.7 us (94%)
  between operations  0.64 us (5%)
    pallas_call x1, Pallas kernels, per_device(): pl.pallas_call(functools.partial(kernel, dims), out_shape=(jax.ShapeDtype...  10.8 us
    pallas_call x1, Pallas kernels, per_device(): pl.pallas_call(write_out, out_shape=(jax.ShapeDtypeStruct(velocity.shape,...  0.92 us

profile of v4, /device:TPU:1, one launch (start us, length us, event | category | flops | bytes accessed | tf_op | source)
XLA Modules:
  0.0 12.4 jit_solution(3417176804924817012)
XLA Ops:
  0.6 10.8 %shard_map.68 = (f32[3,16,16,256]{3,2,1,0:T(8,128)S(1)}, f32[6,16]{1,0:T(8,128)S(1)}) custom-call(f32[3,16,16,256]{3,2,1,0:T(8,128)} %vel.1, f32[6,16,16,256]{3,2,1,0:T(8,128)} %st.1, s32[16,16,256]{2,1,0:T(8,128)} %mat.1, s32[48]{0:T(128)} %order.1, f32[6,4,16]{2,1,0:T(4,128)} %bitcast.2), custom_call_target="tpu_custom_call" | custom-call | tf_op jit(solution)/shard_map/pallas_call | solution.py:388
  11.5 0.9 %shard_map.69 = (f32[3,16,16,256]{3,2,1,0:T(8,128)}, f32[6,16]{1,0:T(8,128)}) custom-call(f32[3,16,16,256]{3,2,1,0:T(8,128)S(1)} %get-tuple-element.6.held, f32[6,16]{1,0:T(8,128)S(1)} %get-tuple-element.7.slip), custom_call_target="tpu_custom_call" | custom-call | tf_op jit(solution)/shard_map/pallas_call | solution.py:419

commit v5 on v4

--- a/solution.py
+++ b/solution.py
@@ -252,25 +252,32 @@
             b = jnp.where(material == index, BUOY[index], b)
         return 0.25 * b
 
-    def plane(x, faces):
-        b = buoyancy(x)
-        sxy, sxz = sx[1, x + 2], sx[2, x + 2]
-        syy, szz, syz = so[0, x], so[1, x], so[2, x]
-        out[0, x] = vb[0, x] + b * (
-            minus(along_x(0, x)) + minus(along_y(sxy)) + minus(z_at(0, sxz, x, faces))
+    def across(x):
+        return minus(along_x(0, x)), plus(along_x(1, x)), plus(along_x(2, x))
+
+    def local(x):
+        sxz, szz, syz = sx[2, x + 2], so[1, x], so[2, x]
+        return (
+            minus(along_y(sx[1, x + 2])) + minus(z_at(0, sxz, x, False)),
+            plus(along_y(so[0, x])) + minus(z_at(1, syz, x, False)),
+            plus(along_y(syz)) + plus(z_at(2, szz, x, False)),
         )
-        out[1, x] = vb[1, x] + b * (
-            plus(along_x(1, x)) + plus(along_y(syy)) + minus(z_at(1, syz, x, faces))
-        )
-        out[2, x] = vb[2, x] + b * (
-            plus(along_x(2, x)) + plus(along_y(syz)) + plus(z_at(2, szz, x, faces))
-        )
-
-    def step(x, carry):
-        plane(x, False)
+
+    def inner(x, carry):
+        b, along, rest = buoyancy(x), across(x), local(x)
+        for c in range(3):
+            out[c, x] = vb[c, x] + b * (along[c] + rest[c])
         return carry
 
-    lax.fori_loop(2, cx - 2, step, 0)
+    def outer(x):
+        b, rest = buoyancy(x), local(x)
+        for c in range(3):
+            out[c, x] = vb[c, x] + b * rest[c]
+
+    edges = (0, 1, cx - 2, cx - 1)
+    lax.fori_loop(2, cx - 2, inner, 0)
+    for x in edges:
+        outer(x)
 
     @pl.when(has_below)
     def _():
@@ -290,7 +297,7 @@
         out[2, x] += b * plus(z_at(2, nothing, x, True))
         return carry
 
-    lax.fori_loop(2, cx - 2, face, 0)
+    lax.fori_loop(0, cx, face, 0)
 
     for k in range(1, n):
         pack_arrival(k).wait_recv()
@@ -322,11 +329,10 @@
         for f in range(3):
             x_copy(f, False).wait_recv()
 
-    def edge(i, carry):
-        plane(i + (cx - 4) * (i // 2), True)
-        return carry
-
-    lax.fori_loop(0, 4, edge, 0)
+    for x in edges:
+        b, along = buoyancy(x), across(x)
+        for c in range(3):
+            out[c, x] += b * along[c]
 
     @pl.when(jnp.logical_and(me >= first_tile, me < first_tile + tiles))
     def _():

time: 12.5 us -> 12.2 us (0.976)
  Pallas kernels: 11.7 us -> 11.4 us
    pallas_call x1, Pallas kernels: 10.8 us -> 10.5 us  [per_device(): pl.pallas_call(functools.partial(kernel, dims), out_shape=(jax.ShapeDtype...]
where the time goes in v5:
time: 12.2 us; the launch traced here: 12.1 us
  Pallas kernels  11.4 us (93%)
  between operations  0.64 us (5%)
    pallas_call x1, Pallas kernels, per_device(): pl.pallas_call(functools.partial(kernel, dims), out_shape=(jax.ShapeDtype...  10.5 us
    pallas_call x1, Pallas kernels, per_device(): pl.pallas_call(write_out, out_shape=(jax.ShapeDtypeStruct(velocity.shape,...  0.92 us

profile of v5, /device:TPU:1, one launch (start us, length us, event | category | flops | bytes accessed | tf_op | source)
XLA Modules:
  0.0 12.1 jit_solution(8205334392120868391)
XLA Ops:
  0.6 10.5 %shard_map.68 = (f32[3,16,16,256]{3,2,1,0:T(8,128)S(1)}, f32[6,16]{1,0:T(8,128)S(1)}) custom-call(f32[3,16,16,256]{3,2,1,0:T(8,128)} %vel.1, f32[6,16,16,256]{3,2,1,0:T(8,128)} %st.1, s32[16,16,256]{2,1,0:T(8,128)} %mat.1, s32[48]{0:T(128)} %order.1, f32[6,4,16]{2,1,0:T(4,128)} %bitcast.2), custom_call_target="tpu_custom_call" | custom-call | tf_op jit(solution)/shard_map/pallas_call | solution.py:394
  11.2 0.9 %shard_map.69 = (f32[3,16,16,256]{3,2,1,0:T(8,128)}, f32[6,16]{1,0:T(8,128)}) custom-call(f32[3,16,16,256]{3,2,1,0:T(8,128)S(1)} %get-tuple-element.6.held, f32[6,16]{1,0:T(8,128)S(1)} %get-tuple-element.7.slip), custom_call_target="tpu_custom_call" | custom-call | tf_op jit(solution)/shard_map/pallas_call | solution.py:425

commit v6 on v5

--- a/solution.py
+++ b/solution.py
@@ -319,6 +319,23 @@
     rate = friction(tau + fields[3], fields[0], fields[1], fields[2])
     slip[...] = rate.T[cx : cx + per]
 
+    inside = jnp.logical_and(me >= first_tile, me < first_tile + tiles)
+
+    def on_fault(rows):
+        @pl.when(inside)
+        def _():
+            for i in rows:
+                s = 0.5 * rate[:, i : i + 1]
+                low = out[0, i, :, row - 128 : row]
+                high = out[0, i, :, row : row + 128]
+                middle = 0.5 * (high + pltpu.roll(low, 1, 1))
+                out[0, i, :, row : row + 128] = jnp.where(lane_one == 0, middle + s, high)
+                out[0, i, :, row - 128 : row] = jnp.where(
+                    lane_one == 127, pltpu.roll(middle, 127, 1) - s, low
+                )
+
+    on_fault(range(2, cx - 2))
+
     @pl.when(has_left)
     def _():
         for f in range(3):
@@ -334,17 +351,7 @@
         for c in range(3):
             out[c, x] += b * along[c]
 
-    @pl.when(jnp.logical_and(me >= first_tile, me < first_tile + tiles))
-    def _():
-        for i in range(cx):
-            s = 0.5 * rate[:, i : i + 1]
-            low = out[0, i, :, row - 128 : row]
-            high = out[0, i, :, row : row + 128]
-            middle = 0.5 * (high + pltpu.roll(low, 1, 1))
-            out[0, i, :, row : row + 128] = jnp.where(lane_one == 0, middle + s, high)
-            out[0, i, :, row - 128 : row] = jnp.where(
-                lane_one == 127, pltpu.roll(middle, 127, 1) - s, low
-            )
+    on_fault(edges)
 
     for k in range(1, n):
         pack_copy(k).wait_send()
@@ -371,8 +378,11 @@
 
 
 def write_out(held, slip, out, slip_out, sem):
-    copies = [pltpu.make_async_copy(slip, slip_out, sem.at[3])]
-    copies += [pltpu.make_async_copy(held.at[c], out.at[c], sem.at[c]) for c in range(3)]
+    copies = [pltpu.make_async_copy(slip, slip_out, sem.at[12])]
+    part = held.shape[1] // 4
+    for i in range(12):
+        at = (i // 4, pl.ds(i % 4 * part, part))
+        copies.append(pltpu.make_async_copy(held.at[at], out.at[at], sem.at[i]))
     for copy in copies:
         copy.start()
     for copy in copies:
@@ -430,7 +440,7 @@
         ),
         in_specs=[resident, resident],
         out_specs=(anywhere, anywhere),
-        scratch_shapes=[dma((4,))],
+        scratch_shapes=[dma((13,))],
         compiler_params=pltpu.CompilerParams(vmem_limit_bytes=4 << 20),
     )(*held)
     return moved, slip.T

time: 12.2 us -> 12.3 us (level)
  no operation moved by 1% of the time
where the time goes in v6:
time: 12.3 us; the launch traced here: 12.1 us
  Pallas kernels  11.5 us (93%)
  between operations  0.64 us (5%)
    pallas_call x1, Pallas kernels, per_device(): pl.pallas_call(functools.partial(kernel, dims), out_shape=(jax.ShapeDtype...  10.5 us
    pallas_call x1, Pallas kernels, per_device(): pl.pallas_call(write_out, out_shape=(jax.ShapeDtypeStruct(velocity.shape,...  0.98 us

profile of v6, /device:TPU:1, one launch (start us, length us, event | category | flops | bytes accessed | tf_op | source)
XLA Modules:
  0.0 12.1 jit_solution(11499266712968349192)
XLA Ops:
  0.6 10.5 %shard_map.68 = (f32[3,16,16,256]{3,2,1,0:T(8,128)S(1)}, f32[6,16]{1,0:T(8,128)S(1)}) custom-call(f32[3,16,16,256]{3,2,1,0:T(8,128)} %vel.1, f32[6,16,16,256]{3,2,1,0:T(8,128)} %st.1, s32[16,16,256]{2,1,0:T(8,128)} %mat.1, s32[48]{0:T(128)} %order.1, f32[6,4,16]{2,1,0:T(4,128)} %bitcast.2), custom_call_target="tpu_custom_call" | custom-call | tf_op jit(solution)/shard_map/pallas_call | solution.py:404
  11.2 1.0 %shard_map.69 = (f32[3,16,16,256]{3,2,1,0:T(8,128)}, f32[6,16]{1,0:T(8,128)}) custom-call(f32[3,16,16,256]{3,2,1,0:T(8,128)S(1)} %get-tuple-element.6.held, f32[6,16]{1,0:T(8,128)S(1)} %get-tuple-element.7.slip), custom_call_target="tpu_custom_call" | custom-call | tf_op jit(solution)/shard_map/pallas_call | solution.py:435

commit v7 on v6

--- a/solution.py
+++ b/solution.py
@@ -136,7 +136,10 @@
     )
 
     def pack_copy(k):
-        peer = lax.rem(me + k, n)
+        down, rise = n - k, k - 1
+        down = down - (down <= me).astype(jnp.int32)
+        rise = rise + (rise >= me).astype(jnp.int32)
+        peer = jnp.where(me < n // 2, down, rise)
         return pltpu.make_async_remote_copy(
             src_ref=packs.at[jnp.clip(peer - first_tile, 0, tiles - 1)],
             dst_ref=recv.at[me],

time: 12.3 us -> 12.3 us (level)
  no operation moved by 1% of the time
where the time goes in v7:
time: 12.3 us; the launch traced here: 12.1 us
  Pallas kernels  11.5 us (93%)
  between operations  0.64 us (5%)
    pallas_call x1, Pallas kernels, per_device(): pl.pallas_call(functools.partial(kernel, dims), out_shape=(jax.ShapeDtype...  10.5 us
    pallas_call x1, Pallas kernels, per_device(): pl.pallas_call(write_out, out_shape=(jax.ShapeDtypeStruct(velocity.shape,...  0.98 us

profile of v7, /device:TPU:1, one launch (start us, length us, event | category | flops | bytes accessed | tf_op | source)
XLA Modules:
  0.0 12.1 jit_solution(10516503839434525994)
XLA Ops:
  0.6 10.5 %shard_map.68 = (f32[3,16,16,256]{3,2,1,0:T(8,128)S(1)}, f32[6,16]{1,0:T(8,128)S(1)}) custom-call(f32[3,16,16,256]{3,2,1,0:T(8,128)} %vel.1, f32[6,16,16,256]{3,2,1,0:T(8,128)} %st.1, s32[16,16,256]{2,1,0:T(8,128)} %mat.1, s32[48]{0:T(128)} %order.1, f32[6,4,16]{2,1,0:T(4,128)} %bitcast.2), custom_call_target="tpu_custom_call" | custom-call | tf_op jit(solution)/shard_map/pallas_call | solution.py:407
  11.2 1.0 %shard_map.69 = (f32[3,16,16,256]{3,2,1,0:T(8,128)}, f32[6,16]{1,0:T(8,128)}) custom-call(f32[3,16,16,256]{3,2,1,0:T(8,128)S(1)} %get-tuple-element.6.held, f32[6,16]{1,0:T(8,128)S(1)} %get-tuple-element.7.slip), custom_call_target="tpu_custom_call" | custom-call | tf_op jit(solution)/shard_map/pallas_call | solution.py:438
